TPU v7x, 256 devices: a whole 4x4x8 slice. The times are simulated.
256 devices in a mesh: dp: 64 (over z_hi, y, x), tensor: 4 (over z_lo, core).
Axes of the slice: x: 4, y: 4, z: 8 (z_hi: 4, z_lo: 2; z = z_hi * 2 + z_lo), core: 2. Of those that a mesh axis runs over, the one named last changes fastest.
Arguments:
- hidden: bfloat16 [32768, 8192], P('dp', 'tensor'), may hold values from -16 to 16
- kv_weight: bfloat16 [8192, 1024], P(None, 'tensor'), may hold values from -0.0625 to 0.0625
- queries: bfloat16 [32768, 4096], P('dp', 'tensor'), may hold values from -28 to 28
- out_grad: bfloat16 [32768, 4096], P('dp', 'tensor'), may hold values from -6 to 6
- live_blocks: int32 [64], P('dp'), may hold values from 0 to 4, as said below
- doc_start: int32 [32768], P('dp'), may hold values from 0 to 127, as said below
Outputs:
- q_grad: bfloat16 [32768, 4096], P('dp', 'tensor')
- hidden_grad: bfloat16 [32768, 8192], P('dp', 'tensor')
- kv_weight_grad: float32 [8192, 1024], P('dp', 'tensor')
Inputs may be any that keep to these rules, and one draw needn't show every extreme that they name: live_blocks[i] + live_blocks[j] = 4 for the two indices i and j of dp that lie half the axis apart; the live blocks of an index are its first ones. doc_start of a row is at most its own position within its block, position 0 of every block is 0, and the rows of one document are consecutive.
All inputs are finite; a program needn't handle non-finite values.
Results may differ from a plain program's by a relative error of at most 0.014.
The roundings to bfloat16 on the way count: a program that leaves them out, or rounds other values in their place, can miss the bound.
Values may be sent and summed in bfloat16 or wider, within the bound.
A program may use at most 128 MiB of HBM per device.

v0:
```python
import jax
import jax.numpy as jnp
from jax import lax
from jax.sharding import PartitionSpec as P

HEAD_DIM = 128
BLOCK = 128
NBLK = 4


def attend(query_rows, key_rows, value_rows, grad_rows, start_rows, live_slots):
    factor = HEAD_DIM ** (-0.5)
    position = jnp.arange(BLOCK)
    allowed = (
        (position[None, None, :] >= start_rows[:, :, None])
        & (position[None, None, :] <= position[None, :, None])
        & live_slots[:, None, None]
    )
    allowed = allowed[:, None, None]
    scores = (
        jnp.einsum("brkgd,bskd->bkgrs", query_rows, key_rows, preferred_element_type=jnp.float32)
        * factor
    )
    row_max = jnp.max(jnp.where(allowed, scores, -1e30), axis=-1, keepdims=True)
    weights = jnp.where(allowed, jnp.exp(scores - row_max), 0.0)
    row_sum = jnp.sum(weights, axis=-1, keepdims=True)
    row_sum = jnp.where(live_slots[:, None, None, None, None], row_sum, 1.0)
    prob_full = weights / row_sum
    prob_low = prob_full.astype(jnp.bfloat16)
    attended = jnp.einsum(
        "bkgrs,bskd->brkgd", prob_low, value_rows, preferred_element_type=jnp.float32
    ).astype(jnp.bfloat16)
    attended = lax.optimization_barrier(attended)
    row_dot = jnp.sum(grad_rows.astype(jnp.float32) * attended.astype(jnp.float32), axis=-1)
    prob_grad = jnp.einsum(
        "brkgd,bskd->bkgrs", grad_rows, value_rows, preferred_element_type=jnp.float32
    )
    score_grad = (
        prob_full * (prob_grad - jnp.transpose(row_dot, (0, 2, 3, 1))[..., None]) * factor
    ).astype(jnp.bfloat16)
    query_grad = jnp.einsum(
        "bkgrs,bskd->brkgd", score_grad, key_rows, preferred_element_type=jnp.float32
    ).astype(jnp.bfloat16)
    key_grad = jnp.einsum(
        "bkgrs,brkgd->bskd", score_grad, query_rows, preferred_element_type=jnp.float32
    ).astype(jnp.bfloat16)
    value_grad = jnp.einsum(
        "bkgrs,brkgd->bskd", prob_low, grad_rows, preferred_element_type=jnp.float32
    ).astype(jnp.bfloat16)
    return (query_grad, jnp.stack([key_grad, value_grad], axis=3))


def on_device(hidden, kv_weight, queries, out_grad, live_blocks, doc_start):
    row_count = hidden.shape[0]
    kv_cols = kv_weight.shape[1]
    kv_local = kv_cols // (2 * HEAD_DIM)
    group_size = queries.shape[1] // (kv_local * HEAD_DIM)
    gathered = lax.all_gather(hidden, "tensor", axis=1, tiled=True)
    key_value = jnp.dot(gathered, kv_weight, preferred_element_type=jnp.float32).astype(
        jnp.bfloat16
    )
    key_value = key_value.reshape(NBLK, BLOCK, kv_local, 2, HEAD_DIM)
    key_rows = key_value[:, :, :, 0]
    value_rows = key_value[:, :, :, 1]
    query_rows = queries.reshape(NBLK, BLOCK, kv_local, group_size, HEAD_DIM)
    grad_rows = out_grad.reshape(NBLK, BLOCK, kv_local, group_size, HEAD_DIM)
    start_rows = doc_start.reshape(NBLK, BLOCK)
    live_count = live_blocks[0]
    query_grad, kv_grad = attend(
        query_rows, key_rows, value_rows, grad_rows, start_rows, jnp.arange(NBLK) < live_count
    )
    q_grad = query_grad.reshape(row_count, queries.shape[1])
    kv_grad = kv_grad.reshape(row_count, kv_cols)
    partial_value = lax.dot_general(
        kv_grad, kv_weight, (((1,), (1,)), ((), ())), preferred_element_type=jnp.float32
    )
    hidden_grad = lax.psum_scatter(
        partial_value.astype(jnp.bfloat16), "tensor", scatter_dimension=1, tiled=True
    )
    weight_grad = lax.psum_scatter(
        lax.dot_general(
            gathered, kv_grad, (((0,), (0,)), ((), ())), preferred_element_type=jnp.float32
        ),
        "dp",
        scatter_dimension=0,
        tiled=True,
    )
    return (q_grad, hidden_grad, weight_grad)


def solution(mesh):
    in_specs = (
        P("dp", "tensor"),
        P(None, "tensor"),
        P("dp", "tensor"),
        P("dp", "tensor"),
        P("dp"),
        P("dp"),
    )
    out_specs = (P("dp", "tensor"), P("dp", "tensor"), P("dp", "tensor"))
    return jax.shard_map(
        on_device, mesh=mesh, in_specs=in_specs, out_specs=out_specs, check_vma=False
    )
```

profile of v0, /device:TPU:1, one launch (start us, length us, event | category | flops | bytes accessed | tf_op | source)
XLA Modules:
  0.0 614.5 jit_solution(17390597814734032298)
XLA Ops:
  7.2 0.0 copy-start.1
  7.2 0.0 copy-start
  7.2 0.0 all-gather.2.cloned.1.call-start
  7.2 0.7 all-gather.2.cloned.1.call-update
  7.9 0.0 reduce-scatter.5.cloned.1.call-start
  8.6 0.0 copy-done.1
  8.6 0.3 copy.48
  8.9 0.0 copy-done
  8.9 1.2 copy.49
  10.2 0.2 convert_bitcast_fusion
  10.4 1.8 copy.50
  12.2 0.0 copy-start.5
  12.2 1.9 copy.26
  14.2 0.0 copy-done.5
  14.2 0.1 fusion.26
  14.3 83.8 %all-gather.2.cloned.1.call-done = bf16[512,8192]{1,0:T(8,128)(2,1)} async-done(((bf16[512,2048]{1,0:T(8,128)(2,1)}), bf16[512,8192]{1,0:T(8,128)(2,1)}) %all-gather.2.cloned.1.call-update) | async-done | bytes 8388624 | tf_op jit(solution)/shard_map/all_gather | solution.py:58
  98.0 7.6 %convolution_convert_fusion.3 = bf16[512,256]{1,0:T(8,128)(2,1)} fusion(bf16[512,8192]{1,0:T(8,128)(2,1)} %all-gather.2.cloned.1.call-done, bf16[8192,256]{1,0:T(8,128)(2,1)} %param.7), kind=kOutput, calls=%fused_computation.20 | convolution fusion | flops 2147614720 | bytes 12845056 | tf_op jit(solution)/shard_map/dot_general | solution.py:59
  105.7 1.0 reshape.122
  106.7 0.4 fusion.31
  107.0 0.0 copy-start.3
  107.1 0.0 copy-start.2
  107.1 0.5 fusion.3
  107.6 0.5 fusion.7
  108.1 0.0 copy-done.3
  108.1 0.1 broadcast_select_fusion
  108.2 0.2 copy-done.2
  108.4 0.7 fusion.13
  109.1 0.8 fusion.8
  110.0 0.3 multiply_reduce_fusion
  110.3 0.0 slice-start
  110.3 0.0 slice-start.1
  110.3 0.9 fusion.10
  111.3 0.4 fusion.14
  111.7 0.3 copy.32
  112.0 0.5 slice-done
  112.5 1.3 slice-done.1
  113.8 5.8 convolution_bitcast_fusion
  119.6 0.0 reduce-scatter.5.cloned.1.call-update
  119.6 0.2 reduce-scatter.3.cloned.1.call-start
  119.8 7.8 %convolution_convert_fusion = bf16[512,8192]{1,0:T(8,128)(2,1)} fusion(bf16[8192,256]{1,0:T(8,128)(2,1)} %param.7, bf16[64,8,2,128]{3,2,1,0:T(2,128)(2,1)S(1)} %bitcast.155), kind=kOutput, calls=%fused_computation | convolution fusion | flops 2151677952 | bytes 12845056 | tf_op jit(solution)/shard_map/dot_general | solution.py:74
  127.6 0.0 reduce-scatter.3.cloned.1.call-update
  127.6 0.9 copy-done.4
  128.6 0.5 fusion.9
  129.1 0.7 copy.29
  129.8 1.2 copy.80
  131.0 353.3 %reduce-scatter.5.cloned.1.call-done = f32[128,256]{0,1:T(8,128)} async-done(((f32[8192,256]{0,1:T(8,128)}), f32[128,256]{0,1:T(8,128)}) %reduce-scatter.5.cloned.1.call-update) | async-done | bytes 131088 | tf_op jit(solution)/shard_map/reduce_scatter | solution.py:80
  484.4 1.7 copy.33
  486.0 122.0 %reduce-scatter.3.cloned.1.call-done = bf16[512,2048]{1,0:T(8,128)(2,1)} async-done(((bf16[512,8192]{1,0:T(8,128)(2,1)}), bf16[512,2048]{1,0:T(8,128)(2,1)}) %reduce-scatter.3.cloned.1.call-update) | async-done | bytes 2097168 | tf_op jit(solution)/shard_map/reduce_scatter | solution.py:77
  (5 shorter events, 0.1 us)
Async XLA Ops:
  7.2 1.4 copy-start.1
  7.2 1.7 copy-start
  7.2 90.9 %all-gather.2.cloned.1.call-start = ((), (), s32[]{:S(2)}) async-start(), calls=%async_computation.2 | async-start | bytes 10485760 | tf_op jit(solution)/shard_map/all_gather | solution.py:58
  7.9 476.4 %reduce-scatter.5.cloned.1.call-start = ((), (), s32[]{:S(2)}) async-start(), calls=%async_computation.4 | async-start | bytes 8519680 | tf_op jit(solution)/shard_map/reduce_scatter | solution.py:80
  12.2 2.0 copy-start.5
  107.0 1.0 copy-start.3
  107.1 1.3 copy-start.2
  110.3 2.2 slice-start
  110.3 3.5 slice-start.1
  119.6 488.4 %reduce-scatter.3.cloned.1.call-start = ((), (), s32[]{:S(2)}) async-start(), calls=%async_computation.3 | async-start | bytes 10485760 | tf_op jit(solution)/shard_map/reduce_scatter | solution.py:77
  127.6 0.9 copy-start.4
Sparse Core Ops, SparseCore 0:
  9.8 88.2 all-gather.1
  119.7 364.6 reduce-scatter.4
  487.6 120.4 reduce-scatter.2
where the time goes:
time: 615 us
  waiting for transfers between devices  560 us (91%)
  matrix products  25.1 us (4%)
  between operations  14.6 us (2%)
  local copies, waits for them, and re-layouts  13.5 us (2%)
    reduce_scatter x1, waiting for transfers between devices, on_device(): lax.psum_scatter(lax.dot_general(gathered, kv_grad, (((0,), (0,)), ((), (...  353 us
    reduce_scatter x1, waiting for transfers between devices, on_device(): lax.psum_scatter(partial_value.astype(jnp.bfloat16), 'tensor', scatter_di...  122 us
    all_gather x1, waiting for transfers between devices, on_device(): gathered = lax.all_gather(hidden, 'tensor', axis=1, tiled=True)  83.8 us
  transfers between devices with their start and end apart: 3, of which 3 were waited for; matrix products, arithmetic and copies ran while one was open for 3% of the time, Pallas kernels for 0%

commit v1 on v0

--- a/solution.py
+++ b/solution.py
@@ -55,7 +55,10 @@
     kv_cols = kv_weight.shape[1]
     kv_local = kv_cols // (2 * HEAD_DIM)
     group_size = queries.shape[1] // (kv_local * HEAD_DIM)
-    gathered = lax.all_gather(hidden, "tensor", axis=1, tiled=True)
+    size = lax.axis_size("tensor")
+    blocks = jnp.stack([hidden for _ in range(size)])
+    blocks = lax.all_to_all(blocks, "tensor", split_axis=0, concat_axis=0)
+    gathered = jnp.concatenate(blocks, axis=1)
     key_value = jnp.dot(gathered, kv_weight, preferred_element_type=jnp.float32).astype(
         jnp.bfloat16
     )

time: 615 us -> 636 us (1.034)
  starting transfers between devices: 0.3 us -> 9.19 us
    all_to_all x0 -> x1, waiting for transfers between devices: none -> 85.6 us  [on_device(): blocks = lax.all_to_all(blocks, 'tensor', split_axis=0, concat_axis=0)]
    all_gather x1 -> x0, waiting for transfers between devices: 83.8 us -> none  [on_device(): gathered = lax.all_gather(hidden, 'tensor', axis=1, tiled=True)]
    all_to_all x0 -> x1, starting transfers between devices: none -> 8.96 us  [on_device(): blocks = lax.all_to_all(blocks, 'tensor', split_axis=0, concat_axis=0)]
where the time goes in v1:
time: 636 us; the launch traced here: 635 us
  waiting for transfers between devices  563 us (89%)
  matrix products  28.4 us (4%)
  local copies, waits for them, and re-layouts  18.6 us (3%)
  between operations  15 us (2%)
  starting transfers between devices  9.19 us (1%)
    reduce_scatter x1, waiting for transfers between devices, on_device(): lax.psum_scatter(lax.dot_general(gathered, kv_grad, (((0,), (0,)), ((), (...  352 us
    reduce_scatter x1, waiting for transfers between devices, on_device(): lax.psum_scatter(partial_value.astype(jnp.bfloat16), 'tensor', scatter_di...  125 us
    all_to_all x1, waiting for transfers between devices, on_device(): blocks = lax.all_to_all(blocks, 'tensor', split_axis=0, concat_axis=0)  85.6 us
  transfers between devices with their start and end apart: 3, of which 3 were waited for; matrix products, arithmetic and copies ran while one was open for 3% of the time, Pallas kernels for 0%

profile of v1, /device:TPU:1, one launch (start us, length us, event | category | flops | bytes accessed | tf_op | source)
XLA Modules:
  0.0 635.3 jit_solution(8112992631194017726)
XLA Ops:
  7.2 2.9 copy.20
  10.0 3.9 stack.16
  13.9 0.0 copy-start.1
  13.9 9.0 %all-to-all-start = ((bf16[4,512,2048]{1,2,0:T(8,128)(2,1)}), bf16[4,512,2048]{1,2,0:T(8,128)(2,1)}, u32[]{:S(2)}, u32[]{:S(2)}) async-start(bf16[4,512,2048]{1,2,0:T(8,128)(2,1)} %stack.16), calls=%async_computation | async-start | bytes 16777216 | tf_op jit(solution)/shard_map/all_to_all | solution.py:60
  22.9 0.0 copy-start
  22.9 0.0 reduce-scatter.5.cloned.1.call-start
  23.6 0.0 copy-done.1
  23.6 0.3 copy.49
  23.9 0.2 copy-done
  24.1 1.2 copy.50
  25.4 0.2 convert_bitcast_fusion
  25.6 1.8 copy.51
  27.4 0.0 copy-start.5
  27.4 1.9 copy.27
  29.4 0.0 copy-done.5
  29.4 0.1 fusion.26
  29.5 85.6 %all-to-all-done = bf16[4,512,2048]{1,2,0:T(8,128)(2,1)} async-done(((bf16[4,512,2048]{1,2,0:T(8,128)(2,1)}), bf16[4,512,2048]{1,2,0:T(8,128)(2,1)}, u32[]{:S(2)}, u32[]{:S(2)}) %all-to-all-start) | async-done | bytes 8388640 | tf_op jit(solution)/shard_map/all_to_all | solution.py:60
  115.1 7.7 %convolution_convert_fusion.3 = bf16[512,256]{1,0:T(8,128)(2,1)} fusion(bf16[512,8192]{0,1:T(8,128)(2,1)} %bitcast.1, bf16[8192,256]{1,0:T(8,128)(2,1)} %param.7), kind=kOutput, calls=%fused_computation.20 | convolution fusion | flops 2147614720 | bytes 12845056 | tf_op jit(solution)/shard_map/dot_general | solution.py:62
  122.8 1.0 reshape.132
  123.8 0.4 fusion.31
  124.2 0.0 copy-start.3
  124.2 0.0 copy-start.2
  124.2 0.5 fusion.3
  124.7 0.5 fusion.7
  125.2 0.0 copy-done.3
  125.2 0.1 broadcast_select_fusion
  125.3 0.2 copy-done.2
  125.5 0.7 fusion.13
  126.2 0.8 fusion.8
  127.1 0.3 multiply_reduce_fusion
  127.4 0.9 fusion.10
  128.4 0.4 fusion.14
  128.8 0.3 copy.33
  129.1 9.0 %convolution_bitcast_fusion = f32[8192,256]{0,1:T(8,128)} fusion(bf16[512,8192]{0,1:T(8,128)(2,1)} %bitcast.1, bf16[64,8,2,128]{3,2,1,0:T(2,128)(2,1)S(1)} %bitcast.155), kind=kOutput, calls=%fused_computation.1 | convolution fusion | flops 2147483648 | bytes 17039360 | tf_op jit(solution)/shard_map/dot_general | solution.py:84
  138.1 0.0 reduce-scatter.5.cloned.1.call-update
  138.1 0.2 reduce-scatter.3.cloned.1.call-start
  138.4 7.8 %convolution_convert_fusion = bf16[512,8192]{1,0:T(8,128)(2,1)} fusion(bf16[8192,256]{1,0:T(8,128)(2,1)} %param.7, bf16[64,8,2,128]{3,2,1,0:T(2,128)(2,1)S(1)} %bitcast.156), kind=kOutput, calls=%fused_computation | convolution fusion | flops 2151677952 | bytes 12845056 | tf_op jit(solution)/shard_map/dot_general | solution.py:77
  146.2 0.0 copy-start.4
  146.2 0.0 reduce-scatter.3.cloned.1.call-update
  146.2 0.9 copy-done.4
  147.1 0.5 fusion.9
  147.6 0.7 copy.30
  148.3 1.2 copy.81
  149.6 351.9 %reduce-scatter.5.cloned.1.call-done = f32[128,256]{0,1:T(8,128)} async-done(((f32[8192,256]{0,1:T(8,128)}), f32[128,256]{0,1:T(8,128)}) %reduce-scatter.5.cloned.1.call-update) | async-done | bytes 131088 | tf_op jit(solution)/shard_map/reduce_scatter | solution.py:83
  501.5 1.7 copy.34
  503.2 125.3 %reduce-scatter.3.cloned.1.call-done = bf16[512,2048]{1,0:T(8,128)(2,1)} async-done(((bf16[512,8192]{1,0:T(8,128)(2,1)}), bf16[512,2048]{1,0:T(8,128)(2,1)}) %reduce-scatter.3.cloned.1.call-update) | async-done | bytes 2097168 | tf_op jit(solution)/shard_map/reduce_scatter | solution.py:80
  (3 shorter events, 0.0 us)
Async XLA Ops:
  13.9 9.7 %copy-start.1 = (bf16[512,1024]{1,0:T(8,128)(2,1)S(1)}, bf16[512,1024]{1,0:T(8,128)(2,1)}, u32[]{:S(2)}) copy-start(bf16[512,1024]{1,0:T(8,128)(2,1)} %param.8) | copy-start | bytes 3145732
  13.9 101.2 %all-to-all-start = ((bf16[4,512,2048]{1,2,0:T(8,128)(2,1)}), bf16[4,512,2048]{1,2,0:T(8,128)(2,1)}, u32[]{:S(2)}, u32[]{:S(2)}) async-start(bf16[4,512,2048]{1,2,0:T(8,128)(2,1)} %stack.16), calls=%async_computation | async-start | bytes 16777216 | tf_op jit(solution)/shard_map/all_to_all | solution.py:60
  22.9 1.2 copy-start
  22.9 478.6 %reduce-scatter.5.cloned.1.call-start = ((), (), s32[]{:S(2)}) async-start(), calls=%async_computation.4 | async-start | bytes 8519680 | tf_op jit(solution)/shard_map/reduce_scatter | solution.py:83
  27.4 2.0 copy-start.5
  124.2 1.0 copy-start.3
  124.2 1.3 copy-start.2
  138.1 490.3 %reduce-scatter.3.cloned.1.call-start = ((), (), s32[]{:S(2)}) async-start(), calls=%async_computation.3 | async-start | bytes 10485760 | tf_op jit(solution)/shard_map/reduce_scatter | solution.py:80
  146.2 0.9 copy-start.4
Sparse Core Ops, SparseCore 0:
  138.3 363.1 reduce-scatter.4
  504.7 123.7 reduce-scatter.2
